TPU v7x, 512 devices: a whole 4x4x16 slice. The times are simulated.
512 devices in a mesh: tok: 32 (over z_hi, y, core), feat: 16 (over x, z_lo).
Axes of the slice: x: 4, y: 4, z: 16 (z_hi: 4, z_lo: 4; z = z_hi * 4 + z_lo), core: 2. Of those that a mesh axis runs over, the one named last changes fastest.
Arguments:
- calib: float32 [5120, 28672], P('tok', 'feat'), may hold values from -6 to 6
- weight: float32 [28672, 512], P('feat', 'tok'), may hold values from -0.03125 to 0.03125
Outputs:
- gram_product: float32 [512, 28672], P('tok', 'feat')
All inputs are finite; a program needn't handle non-finite values.
Results may differ from a plain program's by a relative error of at most 0.000098.
Values sent between devices are 32-bit elements; how exact they have to be, the bound alone decides.
A program may use at most 64 MiB of HBM per device.

v0:
```python
import math

import jax
import jax.numpy as jnp
from jax import lax
from jax.sharding import PartitionSpec as P


def shards(calib, weight):
    tokens_all = calib.shape[0] * lax.axis_size("tok")
    partial_rows = jnp.dot(
        calib,
        lax.all_gather(weight, "tok", axis=1, tiled=True),
        precision=lax.Precision.HIGHEST,
        preferred_element_type=jnp.float32,
    )
    mixed = lax.psum(partial_rows, "feat")
    factor = 1.0 / math.sqrt(tokens_all)
    term = lax.dot_general(
        mixed,
        calib,
        (((0,), (0,)), ((), ())),
        precision=lax.Precision.HIGHEST,
        preferred_element_type=jnp.float32,
    )
    return lax.psum_scatter(term * factor, "tok", scatter_dimension=0, tiled=True)


def solution(mesh):
    return jax.shard_map(
        shards,
        mesh=mesh,
        in_specs=(P("tok", "feat"), P("feat", "tok")),
        out_specs=P("tok", "feat"),
        check_vma=False,
    )
```

profile of v0, /device:TPU:1, one launch (start us, length us, event | category | flops | bytes accessed | tf_op | source)
XLA Modules:
  0.0 422.5 jit_solution(11789714599147911102)
XLA Ops:
  6.5 0.0 copy-start
  6.5 0.0 all-gather.2.cloned.1.call-start
  6.5 0.7 all-gather.2.cloned.1.call-update
  7.3 0.0 all-reduce.2.cloned.1.call-start
  7.3 98.5 %all-gather.2.cloned.1.call-done = f32[1792,512]{0,1:T(8,128)} async-done(((f32[1792,16]{0,1:T(8,128)}), f32[1792,512]{0,1:T(8,128)}) %all-gather.2.cloned.1.call-update) | async-done | bytes 3670032 | tf_op jit(solution)/shard_map/all_gather | solution.py:13
  105.8 0.0 copy-done
  105.8 6.6 %fusion = f32[160,512]{1,0:T(8,128)} fusion(f32[160,1792]{1,0:T(8,128)S(1)} %copy-done, f32[1792,512]{0,1:T(8,128)} %all-gather.2.cloned.1.call-done), kind=kOutput, calls=%fused_computation.1 | convolution fusion | flops 1761607680 | bytes 5144576 | tf_op jit(solution)/shard_map/dot_general | solution.py:11
  112.4 0.0 all-reduce.2.cloned.1.call-update
  112.4 0.0 reduce-scatter.2.cloned.1.call-start
  112.5 152.1 %all-reduce.2.cloned.1.call-done = f32[160,512]{1,0:T(8,128)} async-done(((f32[160,512]{1,0:T(8,128)}), f32[160,512]{1,0:T(8,128)}) %all-reduce.2.cloned.1.call-update) | async-done | bytes 327696 | tf_op jit(solution)/shard_map/psum | solution.py:17
  264.5 5.9 %convolution_multiply_fusion = f32[512,1792]{1,0:T(8,128)} fusion(f32[160,512]{1,0:T(8,128)} %all-reduce.2.cloned.1.call-done, f32[160,1792]{1,0:T(8,128)S(1)} %copy-done), kind=kOutput, calls=%fused_computation | convolution fusion | flops 1762525184 | bytes 5144576 | tf_op jit(solution)/shard_map/dot_general | solution.py:19
  270.4 0.0 reduce-scatter.2.cloned.1.call-update
  270.4 145.5 %reduce-scatter.2.cloned.1.call-done = f32[16,1792]{1,0:T(8,128)} async-done(((f32[512,1792]{1,0:T(8,128)}), f32[16,1792]{1,0:T(8,128)}) %reduce-scatter.2.cloned.1.call-update) | async-done | bytes 114704 | tf_op jit(solution)/shard_map/reduce_scatter | solution.py:26
Async XLA Ops:
  6.5 99.3 %copy-start = (f32[160,1792]{1,0:T(8,128)S(1)}, f32[160,1792]{1,0:T(8,128)}, u32[]{:S(2)}) copy-start(f32[160,1792]{1,0:T(8,128)} %param.2) | copy-start | bytes 3440644
  6.5 99.3 %all-gather.2.cloned.1.call-start = ((), (), s32[]{:S(2)}) async-start(), calls=%async_computation.1 | async-start | bytes 3784704 | tf_op jit(solution)/shard_map/all_gather | solution.py:13
  7.3 257.3 %all-reduce.2.cloned.1.call-start = ((), (), s32[]{:S(2)}) async-start(), calls=%async_computation.2 | async-start | bytes 655360 | tf_op jit(solution)/shard_map/psum | solution.py:17
  112.4 303.5 %reduce-scatter.2.cloned.1.call-start = ((), (), s32[]{:S(2)}) async-start(), calls=%async_computation.3 | async-start | bytes 3784704 | tf_op jit(solution)/shard_map/reduce_scatter | solution.py:26
Sparse Core Ops, SparseCore 0:
  10.5 95.3 all-gather.1
  112.5 151.9 all-reduce.1
  270.5 145.3 reduce-scatter.1
where the time goes:
time: 423 us; the launch traced here: 422 us
  waiting for transfers between devices  397 us (94%)
  between operations  13.1 us (3%)
  matrix products  12.4 us (3%)
    psum x1, waiting for transfers between devices, shards(): mixed = lax.psum(partial_rows, 'feat')  152 us
    reduce_scatter x1, waiting for transfers between devices, shards(): lax.psum_scatter(term * factor, 'tok', scatter_dimension=0, tiled=True)  146 us
    all_gather x1, waiting for transfers between devices, shards(): lax.all_gather(weight, 'tok', axis=1, tiled=True)  98.5 us
  transfers between devices with their start and end apart: 3, of which 3 were waited for; matrix products, arithmetic and copies ran while one was open for 0% of the time, Pallas kernels for 0%

commit v1 on v0

v1 whole, which is shorter than its diff:
```python
import functools
import math

import jax
import jax.numpy as jnp
from jax import lax
from jax.experimental import pallas as pl
from jax.experimental.pallas import tpu as pltpu
from jax.sharding import PartitionSpec as P

MESH = pl.DeviceIdType.MESH
NZ, NY, NC, NX, NL = 4, 4, 2, 4, 4
NP = NX * NC
ORDER = (0, 2, 1, 3)


def split(v):
    hi = v.astype(jnp.bfloat16)
    return hi, (v - hi.astype(jnp.float32)).astype(jnp.bfloat16)


def dot3(a, b, dims):
    (ah, al), (bh, bl) = a, b
    f = lambda p, q: lax.dot_general(
        p, q, (dims, ((), ())), preferred_element_type=jnp.float32
    )
    return f(ah, bh) + (f(ah, bl) + f(al, bh))


def kernel(
    factor,
    calib,
    wt,
    out,
    a,
    ah,
    al,
    g,
    p,
    rs,
    zx,
    m,
    yo,
    yr,
    rz,
    zr,
    loc_sem,
    a_send,
    a_recv,
    w_send,
    w_recv,
    gy_send,
    gy_recv,
    rs_send,
    rs_recv,
    zx_send,
    zx_recv,
    m_send,
    m_recv,
    yr_send,
    yr_recv,
    zr_send,
    zr_recv,
):
    tok, feat = lax.axis_index("tok"), lax.axis_index("feat")
    zh, y, c = tok // (NY * NC), lax.rem(tok, NY * NC) // NC, lax.rem(tok, NC)
    x, zl = feat // NL, lax.rem(feat, NL)
    pm = x * NC + c
    half = calib.shape[1] // NC
    rows = calib.shape[0]
    wide = wt.shape[0]

    def dev(zh=zh, y=y, c=c, x=x, zl=zl):
        return ((zh * NY + y) * NC + c, x * NL + zl)

    def along_z(j, core):
        return dev(zh=lax.rem(zh + j, NZ), c=core)

    def along_y(j):
        return dev(y=lax.rem(y + j, NY))

    def along_l(j):
        return dev(zl=lax.rem(zl + j, NL))

    def piece(j):
        q = lax.rem(pm + j, NP)
        return q, dev(x=q // NC, c=lax.rem(q, NC))

    partner = dev(c=1 - c)

    def send(src, dst, ssem, rsem, to):
        pltpu.make_async_remote_copy(
            src_ref=src,
            dst_ref=dst,
            send_sem=ssem,
            recv_sem=rsem,
            device_id=to,
            device_id_type=MESH,
        ).start()

    def await_bytes(ref, sem):
        pltpu.make_async_copy(ref, ref, sem).wait()

    mine = pl.ds(pl.multiple_of(c * half, 128), half)
    theirs = pl.ds(pl.multiple_of((1 - c) * half, 128), half)
    my_rows = pl.ds(pl.multiple_of(c * rows, 8), rows)
    my_wide = pl.ds(pl.multiple_of(c * wide, 8), wide)

    a_own = pltpu.make_async_copy(calib.at[:, mine], a.at[my_rows], loc_sem.at[0])
    w_own = pltpu.make_async_copy(wt.at[:, mine], g.at[0, y, my_wide], loc_sem.at[1])
    w_own.start()
    a_own.start()

    barrier = pltpu.get_barrier_semaphore()

    def greet(to):
        pl.semaphore_signal(barrier, inc=1, device_id=to, device_id_type=MESH)

    for j in range(1, NZ):
        for k in range(NC):
            greet(along_z(j, k))
    for j in range(1, NY):
        greet(along_y(j))
    for j in range(1, NL):
        greet(along_l(j))
    for j in range(1, NP):
        greet(piece(j)[1])
    pl.semaphore_wait(barrier, (NZ - 1) * NC + (NY - 1) + (NL - 1) + (NP - 1))

    send(wt.at[:, theirs], g.at[0, y, my_wide], w_send.at[0], w_recv.at[0], partner)
    for j in (2, 1, 3):
        for k in range(NC):
            send(
                wt.at[:, pl.ds(k * half, half)],
                g.at[NZ - j, y, my_wide],
                w_send.at[j],
                w_recv.at[NZ - j],
                along_z(j, k),
            )
    send(calib.at[:, theirs], a.at[my_rows], a_send, a_recv, partner)

    def forward(d):
        if d == 0:
            w_own.wait()
            await_bytes(g.at[0, y, my_wide], w_recv.at[0])
        else:
            await_bytes(g.at[d, y], w_recv.at[d])
        for j in range(1, NY):
            send(g.at[d, y], g.at[d, y], gy_send.at[d], gy_recv.at[d], along_y(j))

    def s1(d):
        await_bytes(g.at[d, pl.ds(0, NY - 1)], gy_recv.at[d])
        w = split(g[d].reshape(NY * NC * wide, half))
        acc = dot3((ah[...], al[...]), w, ((1,), (1,)))
        p[d] = acc.reshape(p.shape[1:])

        def one(j, _):
            q, to = piece(j)
            send(p.at[d, q], rs.at[d, j - 1], rs_send.at[d], rs_recv.at[d], to)
            return 0

        lax.fori_loop(1, NP, one, 0)

    def s2(d):
        await_bytes(rs.at[d], rs_recv.at[d])
        acc = p[d, pm]
        for j in range(NP - 1):
            acc = acc + rs[d, j]
        zx[d, zl] = acc
        for j in range(1, NL):
            send(zx.at[d, zl], zx.at[d, zl], zx_send.at[d], zx_recv.at[d], along_l(j))

    def s3(d):
        await_bytes(zx.at[d, pl.ds(0, NL - 1)], zx_recv.at[d])
        acc = zx[d, 0]
        for j in range(1, NL):
            acc = acc + zx[d, j]
        m[d, pm] = acc * factor

        def one(j, _):
            send(m.at[d, pm], m.at[d, pm], m_send.at[d], m_recv.at[d], piece(j)[1])
            return 0

        lax.fori_loop(1, NP, one, 0)

    def s4(d):
        await_bytes(m.at[d, pl.ds(0, NP - 1)], m_recv.at[d])
        v = split(m[d].reshape(NC * rows, NY * NC * wide))
        acc = dot3(v, (ah[...], al[...]), ((0,), (0,)))
        yo[d] = acc.reshape(yo.shape[1:])
        for j in range(1, NY):
            send(
                yo.at[d, lax.rem(y + j, NY)],
                yr.at[d, j - 1],
                yr_send.at[d],
                yr_recv.at[d],
                along_y(j),
            )

    def s5(d):
        await_bytes(yr.at[d], yr_recv.at[d])
        acc = yo[d, y]
        for j in range(NY - 1):
            acc = acc + yr[d, j]
        rz[d] = acc.reshape(rz.shape[1:])
        if d == 0:
            send(rz.at[0, 1 - c], zr.at[0, c], zr_send.at[0], zr_recv.at[0], partner)
        else:
            for k in range(NC):
                send(
                    rz.at[d, k],
                    zr.at[d, c],
                    zr_send.at[d],
                    zr_recv.at[d],
                    along_z(d, k),
                )

    forward(0)
    a_own.wait()
    await_bytes(a.at[my_rows], a_recv)
    hi, lo = split(a[...])
    ah[...] = hi
    al[...] = lo
    s1(0)
    s2(0)
    forward(2)
    forward(1)
    s3(0)
    forward(3)
    s1(2)
    s4(0)
    s1(1)
    s2(2)
    s1(3)
    s2(1)
    s5(0)
    s3(2)
    s2(3)
    s4(2)
    s3(1)
    s4(1)
    s3(3)
    s5(2)
    s4(3)
    s5(1)
    s5(3)

    zr[0, c] = rz[0, c]
    await_bytes(zr.at[0, 0], zr_recv.at[0])
    for d in range(1, NZ):
        await_bytes(zr.at[d], zr_recv.at[d])
    for k in range(NC):
        acc = zr[0, k]
        for d in range(1, NZ):
            acc = acc + zr[d, k]
        out[:, k * half : (k + 1) * half] = acc

    await_bytes(a.at[my_rows], a_send)
    await_bytes(g.at[0, y, my_wide], w_send.at[0])
    await_bytes(zr.at[0, 0], zr_send.at[0])
    for d in range(NZ):
        if d:
            await_bytes(g.at[d, y], w_send.at[d])
            await_bytes(zr.at[d], zr_send.at[d])
        await_bytes(g.at[d, pl.ds(0, NY - 1)], gy_send.at[d])
        await_bytes(rs.at[d], rs_send.at[d])
        await_bytes(zx.at[d, pl.ds(0, NL - 1)], zx_send.at[d])
        await_bytes(m.at[d, pl.ds(0, NP - 1)], m_send.at[d])
        await_bytes(yr.at[d], yr_send.at[d])


def shards(calib, weight):
    rows, feats = calib.shape
    wide = weight.shape[1]
    half = feats // NC
    part = NC * rows // NP
    f32, bf16 = jnp.float32, jnp.bfloat16
    cols = NY * NC * wide
    factor = 1.0 / math.sqrt(rows * lax.axis_size("tok"))
    dma = lambda *n: pltpu.SemaphoreType.DMA(n)
    return pl.pallas_call(
        functools.partial(kernel, factor),
        out_shape=jax.ShapeDtypeStruct((wide, feats), f32),
        in_specs=[pl.BlockSpec(memory_space=pl.ANY)] * 2,
        out_specs=pl.BlockSpec(memory_space=pltpu.VMEM),
        scratch_shapes=[
            pltpu.VMEM((NC * rows, half), f32),
            pltpu.VMEM((NC * rows, half), bf16),
            pltpu.VMEM((NC * rows, half), bf16),
            pltpu.VMEM((NZ, NY, NC * wide, half), f32),
            pltpu.VMEM((NZ, NP, part, cols), f32),
            pltpu.VMEM((NZ, NP - 1, part, cols), f32),
            pltpu.VMEM((NZ, NL, part, cols), f32),
            pltpu.VMEM((NZ, NP, part, cols), f32),
            pltpu.VMEM((NZ, NY, NC * wide, half), f32),
            pltpu.VMEM((NZ, NY - 1, NC * wide, half), f32),
            pltpu.VMEM((NZ, NC, wide, half), f32),
            pltpu.VMEM((NZ, NC, wide, half), f32),
            dma(2),
            pltpu.SemaphoreType.DMA,
            pltpu.SemaphoreType.DMA,
            *[dma(NZ) for _ in range(14)],
        ],
        compiler_params=pltpu.CompilerParams(
            collective_id=0,
            has_side_effects=True,
            vmem_limit_bytes=48 * 1024 * 1024,
        ),
        name="gram",
    )(calib, weight.T)


def solution(mesh):
    return jax.shard_map(
        shards,
        mesh=mesh,
        in_specs=(P("tok", "feat"), P("feat", "tok")),
        out_specs=P("tok", "feat"),
        check_vma=False,
    )
```

time: 423 us -> 95.4 us (0.23)
  the two profiles are of different devices: /device:TPU:1 before, /device:TPU:89 now
where the time goes in v1:
time: 95.4 us; the launch traced here: 95.2 us
  Pallas kernels  92.4 us (97%)
  local copies, waits for them, and re-layouts  2.8 us (3%)
    pallas_call x1, Pallas kernels, shards(): pl.pallas_call(functools.partial(kernel, factor), out_shape=jax.ShapeDtyp...  92.4 us
    unnamed x5, local copies, waits for them, and re-layouts  2.8 us

profile of v1, /device:TPU:89, one launch (start us, length us, event | category | flops | bytes accessed | tf_op | source)
XLA Modules:
  0.0 95.2 jit_solution(17174228715329050323)
XLA Ops:
  0.0 0.0 copy-start
  0.0 1.3 %copy-done = f32[160,1792]{1,0:T(8,128)S(1)} copy-done((f32[160,1792]{1,0:T(8,128)S(1)}, f32[160,1792]{1,0:T(8,128)}, u32[]{:S(2)}) %copy-start) | copy-done | bytes 1146904
  1.3 0.0 copy-start.1
  1.3 0.9 copy-done.1
  2.2 92.4 %gram.1 = f32[16,1792]{1,0:T(8,128)S(1)} custom-call(f32[160,1792]{1,0:T(8,128)S(1)} %copy-done, f32[16,1792]{1,0:T(8,128)S(1)} %bitcast.1), custom_call_target="tpu_custom_call" | custom-call | tf_op jit(solution)/shard_map/gram/pallas_call | solution.py:281
  94.6 0.6 copy.4
Async XLA Ops:
  0.0 1.3 %copy-start = (f32[160,1792]{1,0:T(8,128)S(1)}, f32[160,1792]{1,0:T(8,128)}, u32[]{:S(2)}) copy-start(f32[160,1792]{1,0:T(8,128)} %calib.1) | copy-start | bytes 3440644
  1.3 0.9 copy-start.1

commit v2 on v1

v2 whole, which is shorter than its diff:
```python
import functools
import math

import jax
import jax.numpy as jnp
from jax import lax
from jax.experimental import pallas as pl
from jax.experimental.pallas import tpu as pltpu
from jax.sharding import PartitionSpec as P

MESH = pl.DeviceIdType.MESH
NZ, NY, NC, NX, NL = 4, 4, 2, 4, 4
NP = NX * NC
SUB = 8


STEPS = (
    (0, 0), (0, 1), (1, 0), (0, 2), (1, 1), (2, 0), (0, 3), (1, 2),
    (2, 1), (3, 0), (1, 3), (2, 2), (3, 1), (4, 0), (2, 3), (3, 2),
    (4, 1), (5, 0), (3, 3), (4, 2), (5, 1), (4, 3), (5, 2), (5, 3),
)


def split(v):
    hi = v.astype(jnp.bfloat16)
    return hi, (v - hi.astype(jnp.float32)).astype(jnp.bfloat16)


def dot3(a, b, dims):
    (ah, al), (bh, bl) = a, b
    f = lambda p, q: lax.dot_general(
        p, q, (dims, ((), ())), preferred_element_type=jnp.float32
    )
    return f(ah, bh) + (f(ah, bl) + f(al, bh))


def kernel(
    factor,
    calib,
    wt,
    out,
    a,
    ah,
    al,
    g,
    p,
    rs,
    zx,
    m,
    yo,
    yr,
    rz,
    zr,
    loc_sem,
    a_send,
    a_recv,
    wp_send,
    wp_recv,
    go_send,
    go_recv,
    w_send,
    w_recv,
    gy_send,
    gy_recv,
    rs_send,
    rs_recv,
    zx_send,
    zx_recv,
    m_send,
    m_recv,
    yr_send,
    yr_recv,
    zr_send,
    zp_send,
    zr_recv,
):
    tok, feat = lax.axis_index("tok"), lax.axis_index("feat")
    zh, y, c = tok // (NY * NC), lax.rem(tok, NY * NC) // NC, lax.rem(tok, NC)
    x, zl = feat // NL, lax.rem(feat, NL)
    pm = x * NC + c
    half = calib.shape[1] // NC
    rows = calib.shape[0]
    per = wt.shape[0]
    chunks = NC * per

    def dev(zh=zh, y=y, c=c, x=x, zl=zl):
        return ((zh * NY + y) * NC + c, x * NL + zl)

    def along_z(j, core):
        return dev(zh=lax.rem(zh + j, NZ), c=core)

    def along_y(j):
        return dev(y=lax.rem(y + j, NY))

    def along_l(j):
        return dev(zl=lax.rem(zl + j, NL))

    def piece(j):
        q = lax.rem(pm + j, NP)
        return q, dev(x=q // NC, c=lax.rem(q, NC))

    partner = dev(c=1 - c)

    def send(src, dst, ssem, rsem, to):
        pltpu.make_async_remote_copy(
            src_ref=src,
            dst_ref=dst,
            send_sem=ssem,
            recv_sem=rsem,
            device_id=to,
            device_id_type=MESH,
        ).start()

    def await_bytes(ref, sem):
        pltpu.make_async_copy(ref, ref, sem).wait()

    mine = pl.ds(pl.multiple_of(c * half, 128), half)
    theirs = pl.ds(pl.multiple_of((1 - c) * half, 128), half)
    my_rows = pl.ds(pl.multiple_of(c * rows, 8), rows)
    my_chunks = pl.ds(c * per, per)

    a_own = pltpu.make_async_copy(calib.at[:, mine], a.at[my_rows], loc_sem.at[0])
    w_own = pltpu.make_async_copy(
        wt.at[:, :, mine], g.at[my_chunks, y, 0], loc_sem.at[1]
    )
    w_own.start()
    a_own.start()

    barrier = pltpu.get_barrier_semaphore()

    def greet(to):
        pl.semaphore_signal(barrier, inc=1, device_id=to, device_id_type=MESH)

    for j in range(1, NZ):
        for k in range(NC):
            greet(along_z(j, k))
    for j in range(1, NY):
        greet(along_y(j))
    for j in range(1, NL):
        greet(along_l(j))
    for j in range(1, NP):
        greet(piece(j)[1])
    pl.semaphore_wait(barrier, (NZ - 1) * NC + (NY - 1) + (NL - 1) + (NP - 1))

    send(wt.at[:, :, theirs], g.at[my_chunks, y, 0], wp_send, wp_recv, partner)
    w_own.wait()
    await_bytes(g.at[my_chunks, y, 0], wp_recv)
    for q in range(chunks):
        for j in (2, 1, 3):
            send(
                g.at[q, y, 0],
                g.at[q, y, NZ - j],
                w_send.at[q],
                w_recv.at[q],
                along_z(j, c),
            )
    for j in range(1, NY):
        send(g.at[:, y, 0], g.at[:, y, 0], go_send, go_recv, along_y(j))
    send(calib.at[:, theirs], a.at[my_rows], a_send, a_recv, partner)

    def forward(q):
        got = g.at[q, y, pl.ds(1, NZ - 1)]
        await_bytes(got, w_recv.at[q])
        for j in range(1, NY):
            send(got, got, gy_send.at[q], gy_recv.at[q], along_y(j))

    def s1(q):
        if q == 0:
            await_bytes(g.at[0, pl.ds(0, NY - 1)], go_recv)
        await_bytes(g.at[q, pl.ds(0, NY - 1), pl.ds(0, NZ - 1)], gy_recv.at[q])
        w = split(g[q].reshape(NY * NZ * SUB, half))
        acc = dot3((ah[...], al[...]), w, ((1,), (1,)))
        p[q] = acc.reshape(p.shape[1:])

        def one(j, _):
            t, to = piece(j)
            send(p.at[q, t], rs.at[q, j - 1], rs_send.at[q], rs_recv.at[q], to)
            return 0

        lax.fori_loop(1, NP, one, 0)

    def s2(q):
        await_bytes(rs.at[q], rs_recv.at[q])
        acc = p[q, pm]
        for j in range(NP - 1):
            acc = acc + rs[q, j]
        zx[q, zl] = acc
        for j in range(1, NL):
            send(zx.at[q, zl], zx.at[q, zl], zx_send.at[q], zx_recv.at[q], along_l(j))

    def s3(q):
        await_bytes(zx.at[q, pl.ds(0, NL - 1)], zx_recv.at[q])
        acc = zx[q, 0]
        for j in range(1, NL):
            acc = acc + zx[q, j]
        m[q, pm] = acc * factor

        def one(j, _):
            send(m.at[q, pm], m.at[q, pm], m_send.at[q], m_recv.at[q], piece(j)[1])
            return 0

        lax.fori_loop(1, NP, one, 0)

    def s4(q):
        await_bytes(m.at[q, pl.ds(0, NP - 1)], m_recv.at[q])
        v = split(m[q].reshape(NC * rows, NY * NZ * SUB))
        acc = dot3(v, (ah[...], al[...]), ((0,), (0,)))
        yo[q] = acc.reshape(yo.shape[1:])
        for j in range(1, NY):
            send(
                yo.at[q, lax.rem(y + j, NY)],
                yr.at[q, j - 1],
                yr_send.at[q],
                yr_recv.at[q],
                along_y(j),
            )

    def s5(q):
        await_bytes(yr.at[q], yr_recv.at[q])
        acc = yo[q, y]
        for j in range(NY - 1):
            acc = acc + yr[q, j]
        rz[q] = acc
        owner, i = q // per, q % per
        for d in (2, 1, 3):
            send(
                rz.at[q, d],
                zr.at[i, c * NZ + d],
                zr_send.at[q],
                zr_recv.at[i],
                along_z(d, owner),
            )

        @pl.when(c == owner)
        def _():
            zr[i, c * NZ] = acc[0]

        @pl.when(c != owner)
        def _():
            send(rz.at[q, 0], zr.at[i, c * NZ], zp_send.at[i], zr_recv.at[i], partner)

    a_own.wait()
    await_bytes(a.at[my_rows], a_recv)
    hi, lo = split(a[...])
    ah[...] = hi
    al[...] = lo
    for stage, q in STEPS:
        (forward, s1, s2, s3, s4, s5)[stage](q)

    for i in range(per):
        await_bytes(zr.at[i, pl.ds(0, NC * NZ - 1)], zr_recv.at[i])
        for k in range(NC):
            acc = zr[i, k * NZ]
            for d in range(1, NZ):
                acc = acc + zr[i, k * NZ + d]
            out[i * SUB : (i + 1) * SUB, k * half : (k + 1) * half] = acc

    await_bytes(a.at[my_rows], a_send)
    await_bytes(g.at[my_chunks, y, 0], wp_send)
    await_bytes(g.at[0, pl.ds(0, NY - 1)], go_send)
    for i in range(per):
        await_bytes(rz.at[0, 0], zp_send.at[i])
    for q in range(chunks):
        await_bytes(g.at[q, y, pl.ds(1, NZ - 1)], w_send.at[q])
        await_bytes(g.at[q, pl.ds(0, NY - 1), pl.ds(0, NZ - 1)], gy_send.at[q])
        await_bytes(rs.at[q], rs_send.at[q])
        await_bytes(zx.at[q, pl.ds(0, NL - 1)], zx_send.at[q])
        await_bytes(m.at[q, pl.ds(0, NP - 1)], m_send.at[q])
        await_bytes(yr.at[q], yr_send.at[q])
        await_bytes(rz.at[q, pl.ds(1, NZ - 1)], zr_send.at[q])


def shards(calib, weight):
    rows, feats = calib.shape
    wide = weight.shape[1]
    half = feats // NC
    part = NC * rows // NP
    per = wide // SUB
    q = NC * per
    f32, bf16 = jnp.float32, jnp.bfloat16
    cols = NY * NZ * SUB
    factor = 1.0 / math.sqrt(rows * lax.axis_size("tok"))
    dma = lambda *n: pltpu.SemaphoreType.DMA(n)
    return pl.pallas_call(
        functools.partial(kernel, factor),
        out_shape=jax.ShapeDtypeStruct((wide, feats), f32),
        in_specs=[pl.BlockSpec(memory_space=pl.ANY)] * 2,
        out_specs=pl.BlockSpec(memory_space=pltpu.VMEM),
        scratch_shapes=[
            pltpu.VMEM((NC * rows, half), f32),
            pltpu.VMEM((NC * rows, half), bf16),
            pltpu.VMEM((NC * rows, half), bf16),
            pltpu.VMEM((q, NY, NZ, SUB, half), f32),
            pltpu.VMEM((q, NP, part, cols), f32),
            pltpu.VMEM((q, NP - 1, part, cols), f32),
            pltpu.VMEM((q, NL, part, cols), f32),
            pltpu.VMEM((q, NP, part, cols), f32),
            pltpu.VMEM((q, NY, NZ, SUB, half), f32),
            pltpu.VMEM((q, NY - 1, NZ, SUB, half), f32),
            pltpu.VMEM((q, NZ, SUB, half), f32),
            pltpu.VMEM((per, NC * NZ, SUB, half), f32),
            dma(2),
            *[pltpu.SemaphoreType.DMA] * 6,
            *[dma(q) for _ in range(13)],
            dma(per),
            dma(per),
        ],
        compiler_params=pltpu.CompilerParams(
            collective_id=0,
            has_side_effects=True,
        ),
        name="gram",
    )(calib, weight.T.reshape(per, SUB, feats))


def solution(mesh):
    return jax.shard_map(
        shards,
        mesh=mesh,
        in_specs=(P("tok", "feat"), P("feat", "tok")),
        out_specs=P("tok", "feat"),
        check_vma=False,
    )
```

time: 95.4 us -> 91.3 us (0.957)
  the two profiles are of different devices: /device:TPU:89 before, /device:TPU:1 now
where the time goes in v2:
time: 91.3 us; the launch traced here: 91.2 us
  Pallas kernels  89.6 us (98%)
  local copies, waits for them, and re-layouts  1.55 us (2%)
    pallas_call x1, Pallas kernels, shards(): pl.pallas_call(functools.partial(kernel, factor), out_shape=jax.ShapeDtyp...  89.6 us

profile of v2, /device:TPU:1, one launch (start us, length us, event | category | flops | bytes accessed | tf_op | source)
XLA Modules:
  0.0 91.2 jit_solution(12169095938427309781)
XLA Ops:
  0.0 89.6 %gram.1 = f32[16,1792]{1,0:T(8,128)} custom-call(f32[160,1792]{1,0:T(8,128)} %calib.1, f32[2,8,1792]{2,1,0:T(8,128)} %bitcast.3), custom_call_target="tpu_custom_call" | custom-call | tf_op jit(solution)/shard_map/gram/pallas_call | solution.py:284
  89.6 1.6 %copy.4 = f32[16,1792]{1,0:T(8,128)} copy(f32[16,1792]{1,0:T(8,128)} %gram.1) | data formatting | bytes 229376

commit v3 on v2

v3 whole, which is shorter than its diff:
```python
import functools
import math

import jax
import jax.numpy as jnp
from jax import lax
from jax.experimental import pallas as pl
from jax.experimental.pallas import tpu as pltpu
from jax.sharding import PartitionSpec as P

MESH = pl.DeviceIdType.MESH
NZ, NY, NC, NX, NL = 4, 4, 2, 4, 4
NB = 2
NP = NX * NB
UP, FAR, DOWN = 1, 2, 3
SUB = 8
STEPS = (
    (8, 0), (8, 1), (0, 0), (8, 2), (0, 1), (8, 3), (1, 0), (0, 2),
    (2, 0), (1, 1), (2, 1), (0, 3), (1, 2), (3, 0), (2, 2), (3, 1),
    (1, 3), (4, 0), (2, 3), (3, 2), (4, 1), (5, 0), (3, 3), (4, 2),
    (6, 0), (5, 1), (6, 1), (4, 3), (7, 0), (5, 2), (6, 2), (7, 1),
    (5, 3), (9, 0), (6, 3), (7, 2), (9, 1), (7, 3), (9, 2), (9, 3),
)


def split(v):
    hi = v.astype(jnp.bfloat16)
    return hi, (v - hi.astype(jnp.float32)).astype(jnp.bfloat16)


def dot3(a, b, dims):
    (ah, al), (bh, bl) = a, b
    f = lambda p, q: lax.dot_general(
        p, q, (dims, ((), ())), preferred_element_type=jnp.float32
    )
    return f(ah, bh) + (f(ah, bl) + f(al, bh))


def kernel(
    factor,
    calib,
    wt,
    out,
    a,
    ah,
    al,
    w2,
    g,
    p,
    rs,
    zx,
    m,
    yo,
    yp,
    y1,
    yr,
    rz,
    rl,
    zr,
    loc_sem,
    wp_send,
    wp_recv,
    ao_send,
    an_send,
    a_recv,
    wo_send,
    wo_recv,
    w_send,
    wu_recv,
    wd_recv,
    wr_send,
    wr_recv,
    gp_send,
    gp_recv,
    gy_send,
    gy_recv,
    gb_send,
    gb_recv,
    rs_send,
    rs_recv,
    zx_send,
    zx_recv,
    m_send,
    m_recv,
    yp_send,
    yp_recv,
    yr_send,
    yr_recv,
    zr_send,
    zo_send,
    rl_send,
    rl_recv,
    zr_recv,
):
    tok, feat = lax.axis_index("tok"), lax.axis_index("feat")
    zh, y, c = tok // (NY * NC), lax.rem(tok, NY * NC) // NC, lax.rem(tok, NC)
    x, zl = feat // NL, lax.rem(feat, NL)
    b, pair = lax.rem(y, NB), y // NB
    h = lax.rem(b + pair, 2)
    mate = pair * NB + 1 - b
    near = NY - 1 - y
    yc = pair * NB + c
    yt = jnp.where(h == c, y, mate)
    pm = x * NB + b
    half = calib.shape[1] // 2
    rows = calib.shape[0]
    per = wt.shape[0]
    chunks = NC * per

    def dev(zh=zh, y=y, c=c, x=x, zl=zl):
        return ((zh * NY + y) * NC + c, x * NL + zl)

    def along_z(j):
        return lax.rem(zh + j, NZ)

    def along_l(j):
        return dev(zl=lax.rem(zl + j, NL))

    def piece(j):
        t = lax.rem(pm + j, NP)
        return t, dev(x=t // NB, y=pair * NB + lax.rem(t, NB))

    partner = dev(c=1 - c)

    def send(src, dst, ssem, rsem, to):
        pltpu.make_async_remote_copy(
            src_ref=src,
            dst_ref=dst,
            send_sem=ssem,
            recv_sem=rsem,
            device_id=to,
            device_id_type=MESH,
        ).start()

    def put(src, dst, ssem, rsem, to, here):
        @pl.when(here)
        def _():
            pltpu.make_async_copy(src, dst, rsem).start()

        @pl.when(jnp.logical_not(here))
        def _():
            send(src, dst, ssem, rsem, to)

    def await_bytes(ref, sem):
        pltpu.make_async_copy(ref, ref, sem).wait()

    def half_at(k):
        return pl.ds(pl.multiple_of(k * half, 128), half)

    my_rows = pl.ds(pl.multiple_of(c * rows, 8), rows)
    my_chunks = pl.ds(c * per, per)

    w_own = pltpu.make_async_copy(wt.at[:, :, half_at(c)], w2.at[my_chunks], loc_sem)
    w_own.start()

    barrier = pltpu.get_barrier_semaphore()

    def greet(to):
        pl.semaphore_signal(barrier, inc=1, device_id=to, device_id_type=MESH)

    for j in (1, NZ - 1):
        for k in range(NC):
            greet(dev(zh=along_z(j), c=k))
            greet(dev(zh=along_z(j), y=mate, c=k))
    greet(partner)
    greet(dev(y=mate, c=1 - c))
    greet(dev(y=near))
    for j in range(1, NL):
        greet(along_l(j))
    for j in range(1, NP):
        greet(piece(j)[1])
    pl.semaphore_wait(barrier, 2 * NC * NB + 3 + (NL - 1) + (NP - 1))

    send(wt.at[:, :, half_at(1 - c)], w2.at[my_chunks], wp_send, wp_recv, partner)
    w_own.wait()
    await_bytes(w2.at[my_chunks], wp_recv)
    for q in range(chunks):
        for j, sem in (UP, wu_recv), (DOWN, wd_recv):
            send(
                w2.at[q],
                g.at[q, 0, b, NZ - j],
                w_send.at[q],
                sem.at[q],
                dev(zh=along_z(j), y=yt, c=b),
            )
    w_here = jnp.logical_and(yt == y, b == c)
    put(w2, g.at[:, 0, b, 0], wo_send, wo_recv, dev(y=yt, c=b), w_here)
    a_here = b == c
    put(calib.at[:, half_at(h)], a.at[my_rows], ao_send, a_recv, dev(c=b), a_here)
    send(
        calib.at[:, half_at(1 - h)], a.at[my_rows], an_send, a_recv, dev(y=mate, c=b)
    )

    def onward(q):
        return (UP, wu_recv, wd_recv) if q % 2 == 0 else (DOWN, wd_recv, wu_recv)

    def s8(q):
        j, sem, _ = onward(q)
        got = g.at[q, 0, c, NZ - j]
        await_bytes(got, sem.at[q])
        send(
            got,
            g.at[q, 0, c, FAR],
            wr_send.at[q],
            wr_recv.at[q],
            dev(zh=along_z(j)),
        )

    def s0(q):
        if q == 0:
            await_bytes(w2, wo_recv)
        j, _, sem = onward(q)
        await_bytes(g.at[q, 0, c, j], sem.at[q])
        await_bytes(g.at[q, 0, c, FAR], wr_recv.at[q])
        got = g.at[q, 0, c]
        send(got, g.at[q, 1, c], gy_send.at[q], gy_recv.at[q], dev(y=near))
        send(got, got, gp_send.at[q], gp_recv.at[q], partner)

    def s1(q):
        got = g.at[q, 1, c]
        await_bytes(got, gy_recv.at[q])
        send(got, got, gb_send.at[q], gb_recv.at[q], partner)

    def s2(q):
        if q == 0:
            await_bytes(a, a_recv)
            hi, lo = split(a[...])
            ah[...] = hi
            al[...] = lo
        await_bytes(g.at[q, 0, 1 - c], gp_recv.at[q])
        await_bytes(g.at[q, 1, 1 - c], gb_recv.at[q])
        w = split(g[q].reshape(NY * NZ * SUB, half))
        acc = dot3((ah[...], al[...]), w, ((1,), (1,)))
        p[q] = acc.reshape(p.shape[1:])

        def one(j, _):
            t, to = piece(j)
            send(p.at[q, t], rs.at[q, j - 1], rs_send.at[q], rs_recv.at[q], to)
            return 0

        lax.fori_loop(1, NP, one, 0)

    def s3(q):
        await_bytes(rs.at[q], rs_recv.at[q])
        acc = p[q, pm]
        for j in range(NP - 1):
            acc = acc + rs[q, j]
        zx[q, zl] = acc
        for j in range(1, NL):
            send(zx.at[q, zl], zx.at[q, zl], zx_send.at[q], zx_recv.at[q], along_l(j))

    def s4(q):
        await_bytes(zx.at[q, pl.ds(0, NL - 1)], zx_recv.at[q])
        acc = zx[q, 0]
        for j in range(1, NL):
            acc = acc + zx[q, j]
        m[q, pm] = acc * factor

        def one(j, _):
            send(m.at[q, pm], m.at[q, pm], m_send.at[q], m_recv.at[q], piece(j)[1])
            return 0

        lax.fori_loop(1, NP, one, 0)

    def s5(q):
        await_bytes(m.at[q, pl.ds(0, NP - 1)], m_recv.at[q])
        v = split(m[q].reshape(NC * rows, NY * NZ * SUB))
        acc = dot3(v, (ah[...], al[...]), ((0,), (0,)))
        yo[q] = acc.reshape(yo.shape[1:])
        send(yo.at[q, :, 1 - c], yp.at[q], yp_send.at[q], yp_recv.at[q], partner)

    def s6(q):
        await_bytes(yp.at[q], yp_recv.at[q])
        y1[q] = yo[q, 1, c] + yp[q, 1]
        send(y1.at[q], yr.at[q], yr_send.at[q], yr_recv.at[q], dev(y=near))

    def s7(q):
        await_bytes(yr.at[q], yr_recv.at[q])
        rz[q] = yo[q, 0, c] + yp[q, 0] + yr[q]
        j, _, _ = onward(q)
        send(
            rz.at[q, FAR], rl.at[q], rl_send.at[q], rl_recv.at[q], dev(zh=along_z(j))
        )
        deliver(q, NZ - j)
        put(
            rz.at[q, 0],
            zr.at[q % per, 3 * h],
            zo_send.at[q],
            zr_recv.at[q % per],
            dev(y=yc, c=q // per),
            jnp.logical_and(yc == y, c == q // per),
        )

    def deliver(q, d):
        send(
            rz.at[q, d],
            zr.at[q % per, 3 * h + (1 if d == UP else 2)],
            zr_send.at[q],
            zr_recv.at[q % per],
            dev(zh=along_z(d), y=yc, c=q // per),
        )

    def s9(q):
        j, _, _ = onward(q)
        await_bytes(rl.at[q], rl_recv.at[q])
        rz[q, j] = rz[q, j] + rl[q]
        deliver(q, j)

    for stage, q in STEPS:
        (s0, s1, s2, s3, s4, s5, s6, s7, s8, s9)[stage](q)

    for i in range(per):
        await_bytes(zr.at[i], zr_recv.at[i])
        for k in range(2):
            acc = zr[i, 3 * k]
            for d in range(1, 3):
                acc = acc + zr[i, 3 * k + d]
            out[i * SUB : (i + 1) * SUB, k * half : (k + 1) * half] = acc

    await_bytes(w2.at[my_chunks], wp_send)
    await_bytes(a.at[my_rows], an_send)

    @pl.when(jnp.logical_not(a_here))
    def _():
        await_bytes(a.at[my_rows], ao_send)

    @pl.when(jnp.logical_not(w_here))
    def _():
        await_bytes(w2, wo_send)

    for q in range(chunks):
        await_bytes(g.at[q, 0, 0, pl.ds(0, 2)], w_send.at[q])
        await_bytes(g.at[q, 0, 0, 0], wr_send.at[q])
        await_bytes(rl.at[q], rl_send.at[q])
        await_bytes(g.at[q, 0, 0], gp_send.at[q])
        await_bytes(g.at[q, 0, 0], gy_send.at[q])
        await_bytes(g.at[q, 0, 0], gb_send.at[q])
        await_bytes(rs.at[q], rs_send.at[q])
        await_bytes(zx.at[q, pl.ds(0, NL - 1)], zx_send.at[q])
        await_bytes(m.at[q, pl.ds(0, NP - 1)], m_send.at[q])
        await_bytes(yp.at[q], yp_send.at[q])
        await_bytes(yr.at[q], yr_send.at[q])
        await_bytes(rz.at[q, pl.ds(0, 2)], zr_send.at[q])

        @pl.when(jnp.logical_not(jnp.logical_and(yc == y, c == q // per)))
        def _():
            await_bytes(rz.at[q, 0], zo_send.at[q])


def shards(calib, weight):
    rows, feats = calib.shape
    wide = weight.shape[1]
    half = feats // 2
    part = NC * rows // NP
    per = wide // SUB
    q = NC * per
    f32, bf16 = jnp.float32, jnp.bfloat16
    cols = NY * NZ * SUB
    factor = 1.0 / math.sqrt(rows * lax.axis_size("tok"))
    dma = lambda *n: pltpu.SemaphoreType.DMA(n)
    return pl.pallas_call(
        functools.partial(kernel, factor),
        out_shape=jax.ShapeDtypeStruct((wide, feats), f32),
        in_specs=[pl.BlockSpec(memory_space=pl.ANY)] * 2,
        out_specs=pl.BlockSpec(memory_space=pltpu.VMEM),
        scratch_shapes=[
            pltpu.VMEM((NC * rows, half), f32),
            pltpu.VMEM((NC * rows, half), bf16),
            pltpu.VMEM((NC * rows, half), bf16),
            pltpu.VMEM((q, SUB, half), f32),
            pltpu.VMEM((q, NY // NB, NB, NZ, SUB, half), f32),
            pltpu.VMEM((q, NP, part, cols), f32),
            pltpu.VMEM((q, NP - 1, part, cols), f32),
            pltpu.VMEM((q, NL, part, cols), f32),
            pltpu.VMEM((q, NP, part, cols), f32),
            pltpu.VMEM((q, NY // NB, NB, NZ, SUB, half), f32),
            pltpu.VMEM((q, NY // NB, NZ, SUB, half), f32),
            pltpu.VMEM((q, NZ, SUB, half), f32),
            pltpu.VMEM((q, NZ, SUB, half), f32),
            pltpu.VMEM((q, NZ, SUB, half), f32),
            pltpu.VMEM((q, SUB, half), f32),
            pltpu.VMEM((per, 2 * 3, SUB, half), f32),
            *[pltpu.SemaphoreType.DMA] * 8,
            *[dma(q) for _ in range(25)],
            dma(per),
        ],
        compiler_params=pltpu.CompilerParams(collective_id=0, has_side_effects=True),
        name="gram",
    )(calib, weight.T.reshape(per, SUB, feats))


def solution(mesh):
    return jax.shard_map(
        shards,
        mesh=mesh,
        in_specs=(P("tok", "feat"), P("feat", "tok")),
        out_specs=P("tok", "feat"),
        check_vma=False,
    )
```

time: 91.3 us -> 86 us (0.942)
  Pallas kernels: 89.6 us -> 84.3 us
    pallas_call x1, Pallas kernels: 89.6 us -> 84.3 us  [shards(): pl.pallas_call(functools.partial(kernel, factor), out_shape=jax.ShapeDtyp...]
where the time goes in v3:
time: 86 us; the launch traced here: 85.9 us
  Pallas kernels  84.3 us (98%)
  local copies, waits for them, and re-layouts  1.55 us (2%)
    pallas_call x1, Pallas kernels, shards(): pl.pallas_call(functools.partial(kernel, factor), out_shape=jax.ShapeDtyp...  84.3 us

profile of v3, /device:TPU:1, one launch (start us, length us, event | category | flops | bytes accessed | tf_op | source)
XLA Modules:
  0.0 85.9 jit_solution(5644721731977687723)
XLA Ops:
  0.0 84.3 %gram.1 = f32[16,1792]{1,0:T(8,128)} custom-call(f32[160,1792]{1,0:T(8,128)} %calib.1, f32[2,8,1792]{2,1,0:T(8,128)} %bitcast.3), custom_call_target="tpu_custom_call" | custom-call | tf_op jit(solution)/shard_map/gram/pallas_call | solution.py:361
  84.3 1.6 %copy.4 = f32[16,1792]{1,0:T(8,128)} copy(f32[16,1792]{1,0:T(8,128)} %gram.1) | data formatting | bytes 229376

commit v4 on v3

--- a/solution.py
+++ b/solution.py
@@ -13,14 +13,23 @@
 NB = 2
 NP = NX * NB
 UP, FAR, DOWN = 1, 2, 3
+SLOT = (0, 1, 3, 2)
 SUB = 8
 STEPS = (
-    (8, 0), (8, 1), (0, 0), (8, 2), (0, 1), (8, 3), (1, 0), (0, 2),
-    (2, 0), (1, 1), (2, 1), (0, 3), (1, 2), (3, 0), (2, 2), (3, 1),
-    (1, 3), (4, 0), (2, 3), (3, 2), (4, 1), (5, 0), (3, 3), (4, 2),
-    (6, 0), (5, 1), (6, 1), (4, 3), (7, 0), (5, 2), (6, 2), (7, 1),
-    (5, 3), (9, 0), (6, 3), (7, 2), (9, 1), (7, 3), (9, 2), (9, 3),
+    (10, 1), (10, 0), (10, 2), (10, 3), (8, 1), (8, 0), (8, 2), (8, 3),
+    (0, 0), (0, 1), (1, 0), (1, 1), (0, 2), (2, 0), (0, 3), (2, 1),
+    (1, 2), (1, 3), (2, 2), (3, 0), (2, 3), (3, 1), (3, 2), (4, 0),
+    (3, 3), (4, 1), (4, 2), (5, 0), (4, 3), (5, 1), (6, 0), (6, 1),
+    (5, 2), (5, 3), (7, 0), (6, 2), (7, 1), (6, 3), (7, 2), (7, 3),
+    (9, 1), (9, 0), (9, 2), (9, 3),
 )
+
+
+def first(stage):
+    return next(q for s, q in STEPS if s == stage)
+
+
+LEAD = sum(1 for k, s in enumerate(STEPS) if all(t[0] == 10 for t in STEPS[: k + 1]))
 
 
 def split(v):
@@ -174,15 +183,18 @@
     send(wt.at[:, :, half_at(1 - c)], w2.at[my_chunks], wp_send, wp_recv, partner)
     w_own.wait()
     await_bytes(w2.at[my_chunks], wp_recv)
-    for q in range(chunks):
+    def s10(q):
         for j, sem in (UP, wu_recv), (DOWN, wd_recv):
             send(
                 w2.at[q],
-                g.at[q, 0, b, NZ - j],
+                g.at[q, 0, b, SLOT[NZ - j]],
                 w_send.at[q],
                 sem.at[q],
                 dev(zh=along_z(j), y=yt, c=b),
             )
+
+    for stage, q in STEPS[:LEAD]:
+        s10(q)
     w_here = jnp.logical_and(yt == y, b == c)
     put(w2, g.at[:, 0, b, 0], wo_send, wo_recv, dev(y=yt, c=b), w_here)
     a_here = b == c
@@ -194,27 +206,31 @@
     def onward(q):
         return (UP, wu_recv, wd_recv) if q % 2 == 0 else (DOWN, wd_recv, wu_recv)
 
+    def share(q, got):
+        dst = g.at[q, 1, c, got]
+        got = g.at[q, 0, c, got]
+        send(got, dst, gy_send.at[q], gy_recv.at[q], dev(y=near))
+        send(got, got, gp_send.at[q], gp_recv.at[q], partner)
+
     def s8(q):
-        j, sem, _ = onward(q)
-        got = g.at[q, 0, c, NZ - j]
+        j, sem, other = onward(q)
+        got = g.at[q, 0, c, SLOT[NZ - j]]
         await_bytes(got, sem.at[q])
         send(
             got,
-            g.at[q, 0, c, FAR],
+            g.at[q, 0, c, SLOT[FAR]],
             wr_send.at[q],
             wr_recv.at[q],
             dev(zh=along_z(j)),
         )
+        if q == first(8):
+            await_bytes(w2, wo_recv)
+        await_bytes(g.at[q, 0, c, SLOT[j]], other.at[q])
+        share(q, pl.ds(0, NZ - 1))
 
     def s0(q):
-        if q == 0:
-            await_bytes(w2, wo_recv)
-        j, _, sem = onward(q)
-        await_bytes(g.at[q, 0, c, j], sem.at[q])
-        await_bytes(g.at[q, 0, c, FAR], wr_recv.at[q])
-        got = g.at[q, 0, c]
-        send(got, g.at[q, 1, c], gy_send.at[q], gy_recv.at[q], dev(y=near))
-        send(got, got, gp_send.at[q], gp_recv.at[q], partner)
+        await_bytes(g.at[q, 0, c, SLOT[FAR]], wr_recv.at[q])
+        share(q, pl.ds(NZ - 1, 1))
 
     def s1(q):
         got = g.at[q, 1, c]
@@ -222,7 +238,7 @@
         send(got, got, gb_send.at[q], gb_recv.at[q], partner)
 
     def s2(q):
-        if q == 0:
+        if q == first(2):
             await_bytes(a, a_recv)
             hi, lo = split(a[...])
             ah[...] = hi
@@ -279,7 +295,7 @@
         rz[q] = yo[q, 0, c] + yp[q, 0] + yr[q]
         j, _, _ = onward(q)
         send(
-            rz.at[q, FAR], rl.at[q], rl_send.at[q], rl_recv.at[q], dev(zh=along_z(j))
+            rz.at[q, SLOT[FAR]], rl.at[q], rl_send.at[q], rl_recv.at[q], dev(zh=along_z(j))
         )
         deliver(q, NZ - j)
         put(
@@ -293,8 +309,8 @@
 
     def deliver(q, d):
         send(
-            rz.at[q, d],
-            zr.at[q % per, 3 * h + (1 if d == UP else 2)],
+            rz.at[q, SLOT[d]],
+            zr.at[q % per, 3 * h + SLOT[d]],
             zr_send.at[q],
             zr_recv.at[q % per],
             dev(zh=along_z(d), y=yc, c=q // per),
@@ -303,11 +319,11 @@
     def s9(q):
         j, _, _ = onward(q)
         await_bytes(rl.at[q], rl_recv.at[q])
-        rz[q, j] = rz[q, j] + rl[q]
+        rz[q, SLOT[j]] = rz[q, SLOT[j]] + rl[q]
         deliver(q, j)
 
-    for stage, q in STEPS:
-        (s0, s1, s2, s3, s4, s5, s6, s7, s8, s9)[stage](q)
+    for stage, q in STEPS[LEAD:]:
+        (s0, s1, s2, s3, s4, s5, s6, s7, s8, s9, s10)[stage](q)
 
     for i in range(per):
         await_bytes(zr.at[i], zr_recv.at[i])

time: 86 us -> 86.9 us (1.010)
  Pallas kernels: 84.3 us -> 85.2 us
    pallas_call x1, Pallas kernels: 84.3 us -> 85.2 us  [shards(): pl.pallas_call(functools.partial(kernel, factor), out_shape=jax.ShapeDtyp...]
where the time goes in v4:
time: 86.9 us; the launch traced here: 86.8 us
  Pallas kernels  85.2 us (98%)
  local copies, waits for them, and re-layouts  1.55 us (2%)
    pallas_call x1, Pallas kernels, shards(): pl.pallas_call(functools.partial(kernel, factor), out_shape=jax.ShapeDtyp...  85.2 us

profile of v4, /device:TPU:1, one launch (start us, length us, event | category | flops | bytes accessed | tf_op | source)
XLA Modules:
  0.0 86.8 jit_solution(13539677220144524821)
XLA Ops:
  0.0 85.2 %gram.1 = f32[16,1792]{1,0:T(8,128)} custom-call(f32[160,1792]{1,0:T(8,128)} %calib.1, f32[2,8,1792]{2,1,0:T(8,128)} %bitcast.3), custom_call_target="tpu_custom_call" | custom-call | tf_op jit(solution)/shard_map/gram/pallas_call | solution.py:377
  85.2 1.6 %copy.4 = f32[16,1792]{1,0:T(8,128)} copy(f32[16,1792]{1,0:T(8,128)} %gram.1) | data formatting | bytes 229376

commit v5 on v4

--- a/solution.py
+++ b/solution.py
@@ -13,15 +13,16 @@
 NB = 2
 NP = NX * NB
 UP, FAR, DOWN = 1, 2, 3
+FARTHEST = (4, 3, 5, 2, 6, 1, 7)
 SLOT = (0, 1, 3, 2)
 SUB = 8
 STEPS = (
-    (10, 1), (10, 0), (10, 2), (10, 3), (8, 1), (8, 0), (8, 2), (8, 3),
-    (0, 0), (0, 1), (1, 0), (1, 1), (0, 2), (2, 0), (0, 3), (2, 1),
-    (1, 2), (1, 3), (2, 2), (3, 0), (2, 3), (3, 1), (3, 2), (4, 0),
-    (3, 3), (4, 1), (4, 2), (5, 0), (4, 3), (5, 1), (6, 0), (6, 1),
-    (5, 2), (5, 3), (7, 0), (6, 2), (7, 1), (6, 3), (7, 2), (7, 3),
-    (9, 1), (9, 0), (9, 2), (9, 3),
+    (10, 0), (10, 1), (10, 2), (10, 3), (8, 0), (8, 1), (0, 0), (8, 2),
+    (8, 3), (0, 1), (1, 0), (2, 0), (0, 2), (1, 1), (2, 1), (0, 3),
+    (1, 2), (2, 2), (3, 0), (1, 3), (2, 3), (3, 1), (4, 0), (3, 2),
+    (4, 1), (5, 0), (3, 3), (4, 2), (6, 0), (5, 1), (4, 3), (6, 1),
+    (5, 2), (6, 2), (7, 0), (5, 3), (6, 3), (7, 1), (9, 0), (7, 2),
+    (7, 3), (9, 1), (9, 2), (9, 3),
 )
 
 
@@ -113,6 +114,7 @@
     pm = x * NB + b
     half = calib.shape[1] // 2
     rows = calib.shape[0]
+    cut = half // 256 * 128 + 128
     per = wt.shape[0]
     chunks = NC * per
 
@@ -203,8 +205,7 @@
         calib.at[:, half_at(1 - h)], a.at[my_rows], an_send, a_recv, dev(y=mate, c=b)
     )
 
-    def onward(q):
-        return (UP, wu_recv, wd_recv) if q % 2 == 0 else (DOWN, wd_recv, wu_recv)
+    ways = ((UP, pl.ds(0, cut)), (DOWN, pl.ds(cut, half - cut)))
 
     def share(q, got):
         dst = g.at[q, 1, c, got]
@@ -213,19 +214,18 @@
         send(got, got, gp_send.at[q], gp_recv.at[q], partner)
 
     def s8(q):
-        j, sem, other = onward(q)
-        got = g.at[q, 0, c, SLOT[NZ - j]]
-        await_bytes(got, sem.at[q])
-        send(
-            got,
-            g.at[q, 0, c, SLOT[FAR]],
-            wr_send.at[q],
-            wr_recv.at[q],
-            dev(zh=along_z(j)),
-        )
+        for (j, lanes), sem in zip(ways, (wu_recv, wd_recv)):
+            got = g.at[q, 0, c, SLOT[NZ - j]]
+            await_bytes(got, sem.at[q])
+            send(
+                got.at[:, lanes],
+                g.at[q, 0, c, SLOT[FAR], :, lanes],
+                wr_send.at[q],
+                wr_recv.at[q],
+                dev(zh=along_z(j)),
+            )
         if q == first(8):
             await_bytes(w2, wo_recv)
-        await_bytes(g.at[q, 0, c, SLOT[j]], other.at[q])
         share(q, pl.ds(0, NZ - 1))
 
     def s0(q):
@@ -249,12 +249,9 @@
         acc = dot3((ah[...], al[...]), w, ((1,), (1,)))
         p[q] = acc.reshape(p.shape[1:])
 
-        def one(j, _):
+        for j in FARTHEST:
             t, to = piece(j)
             send(p.at[q, t], rs.at[q, j - 1], rs_send.at[q], rs_recv.at[q], to)
-            return 0
-
-        lax.fori_loop(1, NP, one, 0)
 
     def s3(q):
         await_bytes(rs.at[q], rs_recv.at[q])
@@ -272,11 +269,8 @@
             acc = acc + zx[q, j]
         m[q, pm] = acc * factor
 
-        def one(j, _):
+        for j in FARTHEST:
             send(m.at[q, pm], m.at[q, pm], m_send.at[q], m_recv.at[q], piece(j)[1])
-            return 0
-
-        lax.fori_loop(1, NP, one, 0)
 
     def s5(q):
         await_bytes(m.at[q, pl.ds(0, NP - 1)], m_recv.at[q])
@@ -293,11 +287,16 @@
     def s7(q):
         await_bytes(yr.at[q], yr_recv.at[q])
         rz[q] = yo[q, 0, c] + yp[q, 0] + yr[q]
-        j, _, _ = onward(q)
-        send(
-            rz.at[q, SLOT[FAR]], rl.at[q], rl_send.at[q], rl_recv.at[q], dev(zh=along_z(j))
-        )
-        deliver(q, NZ - j)
+        for j, lanes in ways:
+            send(
+                rz.at[q, SLOT[FAR], :, lanes],
+                rl.at[q, :, lanes],
+                rl_send.at[q],
+                rl_recv.at[q],
+                dev(zh=along_z(j)),
+            )
+        for j, lanes in ways:
+            deliver(q, NZ - j, lanes)
         put(
             rz.at[q, 0],
             zr.at[q % per, 3 * h],
@@ -307,20 +306,20 @@
             jnp.logical_and(yc == y, c == q // per),
         )
 
-    def deliver(q, d):
+    def deliver(q, d, lanes):
         send(
-            rz.at[q, SLOT[d]],
-            zr.at[q % per, 3 * h + SLOT[d]],
+            rz.at[q, SLOT[d], :, lanes],
+            zr.at[q % per, 3 * h + SLOT[d], :, lanes],
             zr_send.at[q],
             zr_recv.at[q % per],
             dev(zh=along_z(d), y=yc, c=q // per),
         )
 
     def s9(q):
-        j, _, _ = onward(q)
         await_bytes(rl.at[q], rl_recv.at[q])
-        rz[q, SLOT[j]] = rz[q, SLOT[j]] + rl[q]
-        deliver(q, j)
+        for j, lanes in ways:
+            rz[q, SLOT[j], :, lanes] = rz[q, SLOT[j], :, lanes] + rl[q, :, lanes]
+            deliver(q, j, lanes)
 
     for stage, q in STEPS[LEAD:]:
         (s0, s1, s2, s3, s4, s5, s6, s7, s8, s9, s10)[stage](q)
@@ -373,6 +372,7 @@
     f32, bf16 = jnp.float32, jnp.bfloat16
     cols = NY * NZ * SUB
     factor = 1.0 / math.sqrt(rows * lax.axis_size("tok"))
+    in_hbm = lambda v: pltpu.with_memory_space_constraint(v, pltpu.HBM)
     dma = lambda *n: pltpu.SemaphoreType.DMA(n)
     return pl.pallas_call(
         functools.partial(kernel, factor),
@@ -400,9 +400,11 @@
             *[dma(q) for _ in range(25)],
             dma(per),
         ],
-        compiler_params=pltpu.CompilerParams(collective_id=0, has_side_effects=True),
+        compiler_params=pltpu.CompilerParams(
+            collective_id=0, has_side_effects=True, vmem_limit_bytes=48 * 1024 * 1024
+        ),
         name="gram",
-    )(calib, weight.T.reshape(per, SUB, feats))
+    )(in_hbm(calib), in_hbm(weight.T.reshape(per, SUB, feats)))
 
 
 def solution(mesh):

time: 86.9 us -> 81 us (0.932)
  Pallas kernels: 85.2 us -> 80.2 us
  local copies, waits for them, and re-layouts: 1.55 us -> 0.65 us
    pallas_call x1, Pallas kernels: 85.2 us -> 80.2 us  [shards(): pl.pallas_call(functools.partial(kernel, factor), out_shape=jax.ShapeDtyp...]
    unnamed x1, local copies, waits for them, and re-layouts: 1.55 us -> 0.65 us
where the time goes in v5:
time: 81 us; the launch traced here: 80.9 us
  Pallas kernels  80.2 us (99%)
    pallas_call x1, Pallas kernels, shards(): pl.pallas_call(functools.partial(kernel, factor), out_shape=jax.ShapeDtyp...  80.2 us

profile of v5, /device:TPU:1, one launch (start us, length us, event | category | flops | bytes accessed | tf_op | source)
XLA Modules:
  0.0 80.9 jit_solution(2189990212121666931)
XLA Ops:
  0.0 80.2 %gram.1 = f32[16,1792]{1,0:T(8,128)S(1)} custom-call(f32[160,1792]{1,0:T(8,128)} %calib.1, f32[2,8,1792]{2,1,0:T(8,128)} %bitcast.3), custom_call_target="tpu_custom_call" | custom-call | tf_op jit(solution)/shard_map/gram/pallas_call | solution.py:377
  80.2 0.6 copy.4

commit v6 on v5

--- a/solution.py
+++ b/solution.py
@@ -13,13 +13,13 @@
 NB = 2
 NP = NX * NB
 UP, FAR, DOWN = 1, 2, 3
-FARTHEST = (4, 3, 5, 2, 6, 1, 7)
+FARTHEST = (1, 7, 2, 6, 3, 5, 4)
 SLOT = (0, 1, 3, 2)
 SUB = 8
 STEPS = (
-    (10, 0), (10, 1), (10, 2), (10, 3), (8, 0), (8, 1), (0, 0), (8, 2),
-    (8, 3), (0, 1), (1, 0), (2, 0), (0, 2), (1, 1), (2, 1), (0, 3),
-    (1, 2), (2, 2), (3, 0), (1, 3), (2, 3), (3, 1), (4, 0), (3, 2),
+    (10, 0), (10, 1), (10, 2), (10, 3), (8, 0), (8, 1), (1, 0), (8, 2),
+    (0, 0), (8, 3), (1, 1), (0, 1), (2, 0), (1, 2), (0, 2), (2, 1),
+    (1, 3), (0, 3), (2, 2), (3, 0), (2, 3), (3, 1), (4, 0), (3, 2),
     (4, 1), (5, 0), (3, 3), (4, 2), (6, 0), (5, 1), (4, 3), (6, 1),
     (5, 2), (6, 2), (7, 0), (5, 3), (6, 3), (7, 1), (9, 0), (7, 2),
     (7, 3), (9, 1), (9, 2), (9, 3),
@@ -86,6 +86,8 @@
     gy_recv,
     gb_send,
     gb_recv,
+    gf_send,
+    gf_recv,
     rs_send,
     rs_recv,
     zx_send,
@@ -125,7 +127,13 @@
         return lax.rem(zh + j, NZ)
 
     def along_l(j):
-        return dev(zl=lax.rem(zl + j, NL))
+        low = zl < NL // 2
+        to = (
+            jnp.where(low, 1 - zl, 2 * NL - 3 - zl),
+            jnp.where(low, NL - 2, 1),
+            jnp.where(low, NL - 1, 0),
+        )
+        return dev(zl=to[j - 1])
 
     def piece(j):
         t = lax.rem(pm + j, NP)
@@ -160,6 +168,7 @@
 
     my_rows = pl.ds(pl.multiple_of(c * rows, 8), rows)
     my_chunks = pl.ds(c * per, per)
+    most = pl.ds(0, NZ - 1)
 
     w_own = pltpu.make_async_copy(wt.at[:, :, half_at(c)], w2.at[my_chunks], loc_sem)
     w_own.start()
@@ -176,11 +185,12 @@
     greet(partner)
     greet(dev(y=mate, c=1 - c))
     greet(dev(y=near))
+    greet(dev(y=near, c=1 - c))
     for j in range(1, NL):
         greet(along_l(j))
     for j in range(1, NP):
         greet(piece(j)[1])
-    pl.semaphore_wait(barrier, 2 * NC * NB + 3 + (NL - 1) + (NP - 1))
+    pl.semaphore_wait(barrier, 2 * NC * NB + 4 + (NL - 1) + (NP - 1))
 
     send(wt.at[:, :, half_at(1 - c)], w2.at[my_chunks], wp_send, wp_recv, partner)
     w_own.wait()
@@ -206,12 +216,6 @@
     )
 
     ways = ((UP, pl.ds(0, cut)), (DOWN, pl.ds(cut, half - cut)))
-
-    def share(q, got):
-        dst = g.at[q, 1, c, got]
-        got = g.at[q, 0, c, got]
-        send(got, dst, gy_send.at[q], gy_recv.at[q], dev(y=near))
-        send(got, got, gp_send.at[q], gp_recv.at[q], partner)
 
     def s8(q):
         for (j, lanes), sem in zip(ways, (wu_recv, wd_recv)):
@@ -226,14 +230,20 @@
             )
         if q == first(8):
             await_bytes(w2, wo_recv)
-        share(q, pl.ds(0, NZ - 1))
+        got = g.at[q, 0, c, most]
+        send(got, g.at[q, 1, c, most], gy_send.at[q], gy_recv.at[q], dev(y=near))
+        send(got, got, gp_send.at[q], gp_recv.at[q], partner)
 
     def s0(q):
-        await_bytes(g.at[q, 0, c, SLOT[FAR]], wr_recv.at[q])
-        share(q, pl.ds(NZ - 1, 1))
+        got = g.at[q, 0, c, SLOT[FAR]]
+        await_bytes(got, wr_recv.at[q])
+        dst = g.at[q, 1, c, SLOT[FAR]]
+        send(got, dst, gf_send.at[q], gf_recv.at[q], dev(y=near, c=1 - c))
+        send(got, dst, gf_send.at[q], gf_recv.at[q], dev(y=near))
+        send(got, got, gp_send.at[q], gp_recv.at[q], partner)
 
     def s1(q):
-        got = g.at[q, 1, c]
+        got = g.at[q, 1, c, most]
         await_bytes(got, gy_recv.at[q])
         send(got, got, gb_send.at[q], gb_recv.at[q], partner)
 
@@ -244,7 +254,8 @@
             ah[...] = hi
             al[...] = lo
         await_bytes(g.at[q, 0, 1 - c], gp_recv.at[q])
-        await_bytes(g.at[q, 1, 1 - c], gb_recv.at[q])
+        await_bytes(g.at[q, 1, 1 - c, most], gb_recv.at[q])
+        await_bytes(g.at[q, 1, :, SLOT[FAR]], gf_recv.at[q])
         w = split(g[q].reshape(NY * NZ * SUB, half))
         acc = dot3((ah[...], al[...]), w, ((1,), (1,)))
         p[q] = acc.reshape(p.shape[1:])
@@ -259,7 +270,7 @@
         for j in range(NP - 1):
             acc = acc + rs[q, j]
         zx[q, zl] = acc
-        for j in range(1, NL):
+        for j in range(NL - 1, 0, -1):
             send(zx.at[q, zl], zx.at[q, zl], zx_send.at[q], zx_recv.at[q], along_l(j))
 
     def s4(q):
@@ -348,8 +359,9 @@
         await_bytes(g.at[q, 0, 0, 0], wr_send.at[q])
         await_bytes(rl.at[q], rl_send.at[q])
         await_bytes(g.at[q, 0, 0], gp_send.at[q])
-        await_bytes(g.at[q, 0, 0], gy_send.at[q])
-        await_bytes(g.at[q, 0, 0], gb_send.at[q])
+        await_bytes(g.at[q, 0, 0, most], gy_send.at[q])
+        await_bytes(g.at[q, 0, 0, most], gb_send.at[q])
+        await_bytes(g.at[q, 1, :, SLOT[FAR]], gf_send.at[q])
         await_bytes(rs.at[q], rs_send.at[q])
         await_bytes(zx.at[q, pl.ds(0, NL - 1)], zx_send.at[q])
         await_bytes(m.at[q, pl.ds(0, NP - 1)], m_send.at[q])
@@ -397,7 +409,7 @@
             pltpu.VMEM((q, SUB, half), f32),
             pltpu.VMEM((per, 2 * 3, SUB, half), f32),
             *[pltpu.SemaphoreType.DMA] * 8,
-            *[dma(q) for _ in range(25)],
+            *[dma(q) for _ in range(27)],
             dma(per),
         ],
         compiler_params=pltpu.CompilerParams(

time: 81 us -> 81.2 us (level)
  no operation moved by 1% of the time
where the time goes in v6:
time: 81.2 us; the launch traced here: 81.1 us
  Pallas kernels  80.4 us (99%)
    pallas_call x1, Pallas kernels, shards(): pl.pallas_call(functools.partial(kernel, factor), out_shape=jax.ShapeDtyp...  80.4 us

profile of v6, /device:TPU:1, one launch (start us, length us, event | category | flops | bytes accessed | tf_op | source)
XLA Modules:
  0.0 81.1 jit_solution(10333872141446643229)
XLA Ops:
  0.0 80.4 %gram.1 = f32[16,1792]{1,0:T(8,128)S(1)} custom-call(f32[160,1792]{1,0:T(8,128)} %calib.1, f32[2,8,1792]{2,1,0:T(8,128)} %bitcast.3), custom_call_target="tpu_custom_call" | custom-call | tf_op jit(solution)/shard_map/gram/pallas_call | solution.py:389
  80.4 0.6 copy.4

commit v7 on v6

--- a/solution.py
+++ b/solution.py
@@ -13,7 +13,7 @@
 NB = 2
 NP = NX * NB
 UP, FAR, DOWN = 1, 2, 3
-FARTHEST = (1, 7, 2, 6, 3, 5, 4)
+ROUND = (1, 7, 2, 6, 3, 5, 4)
 SLOT = (0, 1, 3, 2)
 SUB = 8
 STEPS = (
@@ -21,8 +21,8 @@
     (0, 0), (8, 3), (1, 1), (0, 1), (2, 0), (1, 2), (0, 2), (2, 1),
     (1, 3), (0, 3), (2, 2), (3, 0), (2, 3), (3, 1), (4, 0), (3, 2),
     (4, 1), (5, 0), (3, 3), (4, 2), (6, 0), (5, 1), (4, 3), (6, 1),
-    (5, 2), (6, 2), (7, 0), (5, 3), (6, 3), (7, 1), (9, 0), (7, 2),
-    (7, 3), (9, 1), (9, 2), (9, 3),
+    (5, 2), (6, 2), (11, 0), (7, 0), (5, 3), (11, 1), (6, 3), (11, 2),
+    (7, 1), (9, 0), (11, 3), (7, 2), (7, 3), (9, 1), (9, 2), (9, 3),
 )
 
 
@@ -96,6 +96,8 @@
     m_recv,
     yp_send,
     yp_recv,
+    yf_send,
+    yf_recv,
     yr_send,
     yr_recv,
     zr_send,
@@ -260,7 +262,7 @@
         acc = dot3((ah[...], al[...]), w, ((1,), (1,)))
         p[q] = acc.reshape(p.shape[1:])
 
-        for j in FARTHEST:
+        for j in ROUND:
             t, to = piece(j)
             send(p.at[q, t], rs.at[q, j - 1], rs_send.at[q], rs_recv.at[q], to)
 
@@ -280,7 +282,7 @@
             acc = acc + zx[q, j]
         m[q, pm] = acc * factor
 
-        for j in FARTHEST:
+        for j in ROUND:
             send(m.at[q, pm], m.at[q, pm], m_send.at[q], m_recv.at[q], piece(j)[1])
 
     def s5(q):
@@ -293,19 +295,26 @@
     def s6(q):
         await_bytes(yp.at[q], yp_recv.at[q])
         y1[q] = yo[q, 1, c] + yp[q, 1]
-        send(y1.at[q], yr.at[q], yr_send.at[q], yr_recv.at[q], dev(y=near))
-
-    def s7(q):
-        await_bytes(yr.at[q], yr_recv.at[q])
-        rz[q] = yo[q, 0, c] + yp[q, 0] + yr[q]
+        far, to = SLOT[FAR], dev(y=near)
+        send(y1.at[q, far], yr.at[q, far], yf_send.at[q], yf_recv.at[q], to)
+        send(y1.at[q, most], yr.at[q, most], yr_send.at[q], yr_recv.at[q], to)
+
+    def s11(q):
+        far = SLOT[FAR]
+        await_bytes(yr.at[q, far], yf_recv.at[q])
+        rz[q, far] = yo[q, 0, c, far] + yp[q, 0, far] + yr[q, far]
         for j, lanes in ways:
             send(
-                rz.at[q, SLOT[FAR], :, lanes],
+                rz.at[q, far, :, lanes],
                 rl.at[q, :, lanes],
                 rl_send.at[q],
                 rl_recv.at[q],
                 dev(zh=along_z(j)),
             )
+
+    def s7(q):
+        await_bytes(yr.at[q, most], yr_recv.at[q])
+        rz[q, most] = yo[q, 0, c, most] + yp[q, 0, most] + yr[q, most]
         for j, lanes in ways:
             deliver(q, NZ - j, lanes)
         put(
@@ -333,7 +342,7 @@
             deliver(q, j, lanes)
 
     for stage, q in STEPS[LEAD:]:
-        (s0, s1, s2, s3, s4, s5, s6, s7, s8, s9, s10)[stage](q)
+        (s0, s1, s2, s3, s4, s5, s6, s7, s8, s9, s10, s11)[stage](q)
 
     for i in range(per):
         await_bytes(zr.at[i], zr_recv.at[i])
@@ -366,7 +375,8 @@
         await_bytes(zx.at[q, pl.ds(0, NL - 1)], zx_send.at[q])
         await_bytes(m.at[q, pl.ds(0, NP - 1)], m_send.at[q])
         await_bytes(yp.at[q], yp_send.at[q])
-        await_bytes(yr.at[q], yr_send.at[q])
+        await_bytes(yr.at[q, SLOT[FAR]], yf_send.at[q])
+        await_bytes(yr.at[q, most], yr_send.at[q])
         await_bytes(rz.at[q, pl.ds(0, 2)], zr_send.at[q])
 
         @pl.when(jnp.logical_not(jnp.logical_and(yc == y, c == q // per)))
@@ -409,7 +419,7 @@
             pltpu.VMEM((q, SUB, half), f32),
             pltpu.VMEM((per, 2 * 3, SUB, half), f32),
             *[pltpu.SemaphoreType.DMA] * 8,
-            *[dma(q) for _ in range(27)],
+            *[dma(q) for _ in range(29)],
             dma(per),
         ],
         compiler_params=pltpu.CompilerParams(

time: 81.2 us -> 80 us (0.985)
  Pallas kernels: 80.4 us -> 78.9 us
    pallas_call x1, Pallas kernels: 80.4 us -> 78.9 us  [shards(): pl.pallas_call(functools.partial(kernel, factor), out_shape=jax.ShapeDtyp...]
where the time goes in v7:
time: 80 us; the launch traced here: 79.5 us
  Pallas kernels  78.9 us (99%)
    pallas_call x1, Pallas kernels, shards(): pl.pallas_call(functools.partial(kernel, factor), out_shape=jax.ShapeDtyp...  78.9 us

profile of v7, /device:TPU:1, one launch (start us, length us, event | category | flops | bytes accessed | tf_op | source)
XLA Modules:
  0.0 79.5 jit_solution(11546788715749388925)
XLA Ops:
  0.0 78.9 %gram.1 = f32[16,1792]{1,0:T(8,128)S(1)} custom-call(f32[160,1792]{1,0:T(8,128)} %calib.1, f32[2,8,1792]{2,1,0:T(8,128)} %bitcast.3), custom_call_target="tpu_custom_call" | custom-call | tf_op jit(solution)/shard_map/gram/pallas_call | solution.py:399
  78.9 0.6 copy.4

commit v8 on v7

--- a/solution.py
+++ b/solution.py
@@ -294,9 +294,10 @@
 
     def s6(q):
         await_bytes(yp.at[q], yp_recv.at[q])
-        y1[q] = yo[q, 1, c] + yp[q, 1]
         far, to = SLOT[FAR], dev(y=near)
+        y1[q, far] = yo[q, 1, c, far] + yp[q, 1, far]
         send(y1.at[q, far], yr.at[q, far], yf_send.at[q], yf_recv.at[q], to)
+        y1[q, most] = yo[q, 1, c, most] + yp[q, 1, most]
         send(y1.at[q, most], yr.at[q, most], yr_send.at[q], yr_recv.at[q], to)
 
     def s11(q):

time: 80 us -> 80 us (level)
  no operation moved by 1% of the time
where the time goes in v8:
time: 80 us; the launch traced here: 79.6 us
  Pallas kernels  78.9 us (99%)
    pallas_call x1, Pallas kernels, shards(): pl.pallas_call(functools.partial(kernel, factor), out_shape=jax.ShapeDtyp...  78.9 us

profile of v8, /device:TPU:1, one launch (start us, length us, event | category | flops | bytes accessed | tf_op | source)
XLA Modules:
  0.0 79.6 jit_solution(9890539083801855288)
XLA Ops:
  0.0 78.9 %gram.1 = f32[16,1792]{1,0:T(8,128)S(1)} custom-call(f32[160,1792]{1,0:T(8,128)} %calib.1, f32[2,8,1792]{2,1,0:T(8,128)} %bitcast.3), custom_call_target="tpu_custom_call" | custom-call | tf_op jit(solution)/shard_map/gram/pallas_call | solution.py:400
  78.9 0.6 copy.4
